TPU v7x, 512 devices: a whole 4x4x16 slice. The times are simulated.
512 devices in a mesh: aux: 128 (over z, x_hi, y), occ: 4 (over x_lo, core).
Axes of the slice: x: 4 (x_hi: 2, x_lo: 2; x = x_hi * 2 + x_lo), y: 4, z: 16, core: 2. Of those that a mesh axis runs over, the one named last changes fastest.
Arguments:
- integrals: bfloat16 [2304, 32, 6144], P('aux', None, 'occ'), may hold values from -6 to 6
- coefficients: bfloat16 [6144, 48], P('occ'), may hold values from -0.29882812 to 0.29882812
- screening: int32 [32, 48], replicated, may hold values 0 or 1
- metric_factor: bfloat16 [2304, 2304], P('aux'), may hold values from -2 to 4
Outputs:
- gamma_block: bfloat16 [2304, 32, 6144], P('aux', 'occ')
All inputs are finite; a program needn't handle non-finite values.
Results may differ from a plain program's by a relative error of at most 0.0057.
Values may be sent and summed in bfloat16 or wider, within the bound.
A program may use at most 64 MiB of HBM per device.

v0:
```python
import jax
import jax.numpy as jnp
from jax import lax
from jax.sharding import PartitionSpec as P

TILE = 128


def on_device(integrals, coefficients, screening, metric_factor):
    aux_dev, rows_all, basis_part = integrals.shape
    occ_count = coefficients.shape[1]
    occ_size = lax.axis_size("occ")
    occ_index = lax.axis_index("occ")
    rows_dev = rows_all // occ_size
    tiles_part = basis_part // TILE
    screen_tiles = screening.astype(jnp.bfloat16)
    part_tiles = lax.dynamic_slice_in_dim(screen_tiles, occ_index * tiles_part, tiles_part, 1)
    part_screen = jnp.repeat(part_tiles, TILE, axis=1)
    masked = integrals * part_screen[None]
    partial_value = jnp.einsum(
        "pmn,ni->pmi", masked, coefficients, preferred_element_type=jnp.float32
    )
    partial_value = partial_value.reshape(aux_dev, rows_all * occ_count)
    half_transformed = lax.psum_scatter(
        partial_value, "occ", scatter_dimension=1, tiled=True
    ).astype(jnp.bfloat16)
    fitted = jnp.dot(
        metric_factor,
        lax.all_gather(half_transformed, "aux", axis=0, tiled=True),
        preferred_element_type=jnp.float32,
    ).astype(jnp.bfloat16)
    whole_coefficients = lax.all_gather(coefficients, "occ", axis=0, tiled=True)
    own_tiles = lax.dynamic_slice_in_dim(screen_tiles, occ_index * rows_dev, rows_dev, 0)
    own_screen = jnp.repeat(own_tiles, TILE, axis=1).astype(jnp.float32)
    flattened = fitted.reshape(aux_dev * rows_dev, occ_count)
    product = lax.dot_general(
        flattened, whole_coefficients, (((1,), (1,)), ((), ())), preferred_element_type=jnp.float32
    )
    product = product.reshape(aux_dev, rows_dev, whole_coefficients.shape[0])
    return (product * own_screen[None]).astype(jnp.bfloat16)


def solution(mesh):
    return jax.shard_map(
        on_device,
        mesh=mesh,
        in_specs=(P("aux", None, "occ"), P("occ", None), P(), P("aux", None)),
        out_specs=P("aux", "occ", None),
        check_vma=False,
    )
```

profile of v0, /device:TPU:8, one launch (start us, length us, event | category | flops | bytes accessed | tf_op | source)
XLA Modules:
  0.0 273.1 jit_solution(12376429188576232641)
XLA Ops:
  6.5 0.0 copy-start
  6.5 0.0 reduce-scatter.2.cloned.1.call-start
  6.5 0.8 convert_element_type.26
  7.3 0.1 constant_dynamic-slice_fusion
  7.4 0.1 broadcast_in_dim.7
  7.5 0.0 copy-start.1
  7.6 2.1 fusion.1
  9.7 0.8 reshape.15
  10.5 0.0 reduce-scatter.2.cloned.1.call-update
  10.6 0.0 all-gather.3.cloned.1.call-start
  10.6 29.2 %reduce-scatter.2.cloned.1.call-done = f32[18,384]{1,0:T(8,128)} async-done(((f32[18,1536]{1,0:T(8,128)}), f32[18,384]{1,0:T(8,128)}) %reduce-scatter.2.cloned.1.call-update) | async-done | bytes 27664 | tf_op jit(solution)/shard_map/reduce_scatter | solution.py:24
  39.8 1.4 convert_bitcast_fusion
  41.1 0.0 all-gather.3.cloned.1.call-update
  41.2 0.1 copy.7
  41.3 0.0 copy-done.1
  41.3 7.7 %all_gather.7 = bf16[6144,48]{0,1:T(8,128)(2,1)S(1)} all-gather(bf16[1536,48]{0,1:T(8,128)(2,1)S(1)} %copy-done.1), channel_id=1, replica_groups=mesh['aux'=128,'occ'=4] {'occ'}, dimensions={0}, use_global_device_ids=true | all-gather | bytes 737280 | tf_op jit(solution)/shard_map/all_gather | solution.py:32
  48.9 0.1 broadcast_bitcast_fusion
  49.0 212.3 %all-gather.3.cloned.1.call-done = bf16[128,18,384]{2,1,0:T(8,128)(2,1)} async-done(((bf16[1,18,384]{2,1,0:T(8,128)(2,1)}), bf16[128,18,384]{2,1,0:T(8,128)(2,1)}) %all-gather.3.cloned.1.call-update) | async-done | bytes 1769488 | tf_op jit(solution)/shard_map/all_gather | solution.py:29
  261.3 2.6 reshape.17
  264.0 0.0 copy-done
  264.0 0.3 fusion.3
  264.3 0.1 dot_general.13
  264.5 1.8 fusion
  (2 shorter events, 0.0 us)
Async XLA Ops:
  6.5 257.4 %copy-start = (bf16[18,2304]{1,0:T(8,128)(2,1)S(1)}, bf16[18,2304]{1,0:T(8,128)(2,1)}, u32[]{:S(2)}) copy-start(bf16[18,2304]{1,0:T(8,128)(2,1)} %param.7) | copy-start | bytes 248836
  6.5 33.2 %reduce-scatter.2.cloned.1.call-start = ((), (), s32[]{:S(2)}) async-start(), calls=%async_computation.1 | async-start | bytes 184320 | tf_op jit(solution)/shard_map/reduce_scatter | solution.py:24
  7.5 33.7 %copy-start.1 = (bf16[1536,48]{0,1:T(8,128)(2,1)S(1)}, bf16[1536,48]{0,1:T(8,128)(2,1)}, u32[]{:S(2)}) copy-start(bf16[1536,48]{0,1:T(8,128)(2,1)} %param.5) | copy-start | bytes 442372
  10.6 250.8 %all-gather.3.cloned.1.call-start = ((), (), s32[]{:S(2)}) async-start(), calls=%async_computation.2 | async-start | bytes 2377728 | tf_op jit(solution)/shard_map/all_gather | solution.py:29
Sparse Core Ops, SparseCore 0:
  10.7 29.0 reduce-scatter.1
  44.2 217.0 all-gather.2
where the time goes:
time: 273 us
  waiting for transfers between devices  241 us (88%)
  between operations  13.5 us (5%)
  blocking collectives  7.67 us (3%)
  matrix products  4.27 us (2%)
  local copies, waits for them, and re-layouts  4.02 us (1%)
    all_gather x1, waiting for transfers between devices, on_device(): lax.all_gather(half_transformed, 'aux', axis=0, tiled=True)  212 us
    reduce_scatter x1, waiting for transfers between devices, on_device(): lax.psum_scatter(partial_value, 'occ', scatter_dimension=1, tiled=True)  29.2 us
    all_gather x1, blocking collectives, on_device(): whole_coefficients = lax.all_gather(coefficients, 'occ', axis=0, tiled=True)  7.67 us
  transfers between devices with their start and end apart: 2, of which 2 were waited for; matrix products, arithmetic and copies ran while one was open for 0% of the time, Pallas kernels for 0%

commit v1 on v0

--- a/solution.py
+++ b/solution.py
@@ -24,10 +24,11 @@
     half_transformed = lax.psum_scatter(
         partial_value, "occ", scatter_dimension=1, tiled=True
     ).astype(jnp.bfloat16)
+    supply_the_skins = lambda local: jnp.concatenate(
+        lax.all_to_all(jnp.stack([local for _ in range(lax.psum(1, "aux"))], 0), "aux", 0, 0), 0
+    )
     fitted = jnp.dot(
-        metric_factor,
-        lax.all_gather(half_transformed, "aux", axis=0, tiled=True),
-        preferred_element_type=jnp.float32,
+        metric_factor, supply_the_skins(half_transformed), preferred_element_type=jnp.float32
     ).astype(jnp.bfloat16)
     whole_coefficients = lax.all_gather(coefficients, "occ", axis=0, tiled=True)
     own_tiles = lax.dynamic_slice_in_dim(screen_tiles, occ_index * rows_dev, rows_dev, 0)

time: 273 us -> 185 us (0.68)
  the two profiles are of different devices: /device:TPU:8 before, /device:TPU:40 now
where the time goes in v1:
time: 185 us; the launch traced here: 184 us
  waiting for transfers between devices  132 us (71%)
  starting transfers between devices  19.1 us (10%)
  between operations  13.5 us (7%)
  blocking collectives  8.08 us (4%)
  local copies, waits for them, and re-layouts  5.63 us (3%)
  matrix products  4.24 us (2%)
    all_to_all x1, waiting for transfers between devices, on_device(): lax.all_to_all(jnp.stack([local for _ in range(lax.psum(1, 'aux'))], 0),...  104 us
    reduce_scatter x1, waiting for transfers between devices, on_device(): lax.psum_scatter(partial_value, 'occ', scatter_dimension=1, tiled=True)  28.9 us
    all_to_all x1, starting transfers between devices, on_device(): lax.all_to_all(jnp.stack([local for _ in range(lax.psum(1, 'aux'))], 0),...  19.1 us
    all_gather x1, blocking collectives, on_device(): whole_coefficients = lax.all_gather(coefficients, 'occ', axis=0, tiled=True)  8.08 us
  transfers between devices with their start and end apart: 2, of which 2 were waited for; matrix products, arithmetic and copies ran while one was open for 0% of the time, Pallas kernels for 0%

profile of v1, /device:TPU:40, one launch (start us, length us, event | category | flops | bytes accessed | tf_op | source)
XLA Modules:
  0.0 184.4 jit_solution(12946130230778986033)
XLA Ops:
  6.5 0.0 copy-start
  6.5 0.0 reduce-scatter.2.cloned.1.call-start
  6.5 0.8 convert_element_type.26
  7.3 0.1 constant_dynamic-slice_fusion
  7.4 0.1 broadcast_in_dim.7
  7.5 2.1 %fusion.1 = f32[18,32,48]{2,1,0:T(8,128)S(1)} fusion(bf16[18,32,1536]{2,1,0:T(8,128)(2,1)} %param.4, bf16[32,1536]{1,0:T(8,128)(2,1)S(1)} %bitcast.18, bf16[1536,48]{0,1:T(8,128)(2,1)} %param.5), kind=kOutput, calls=%fused_computation.2 | convolution fusion | flops 85819392 | bytes 2125824 | tf_op jit(solution)/shard_map/pmn,ni->pmi/dot_general | solution.py:20
  9.6 0.8 reshape.20
  10.5 0.0 reduce-scatter.2.cloned.1.call-update
  10.5 28.9 %reduce-scatter.2.cloned.1.call-done = f32[18,384]{1,0:T(8,128)} async-done(((f32[18,1536]{1,0:T(8,128)}), f32[18,384]{1,0:T(8,128)}) %reduce-scatter.2.cloned.1.call-update) | async-done | bytes 27664 | tf_op jit(solution)/shard_map/reduce_scatter | solution.py:24
  39.4 0.8 convert_element_type.27
  40.1 1.6 stack.2
  41.8 0.0 copy-start.1
  41.8 19.1 %all-to-all-start = ((bf16[128,18,384]{2,1,0:T(8,128)(2,1)}), bf16[128,18,384]{2,1,0:T(8,128)(2,1)}, u32[]{:S(2)}, u32[]{:S(2)}) async-start(bf16[128,18,384]{2,1,0:T(8,128)(2,1)} %stack.2), calls=%async_computation.1 | async-start | bytes 4718592 | tf_op jit(solution)/shard_map/all_to_all | solution.py:28
  60.9 0.1 copy.6
  60.9 0.0 copy-done.1
  60.9 8.1 %all_gather.3 = bf16[6144,48]{0,1:T(8,128)(2,1)S(1)} all-gather(bf16[1536,48]{0,1:T(8,128)(2,1)S(1)} %copy-done.1), channel_id=1, replica_groups=mesh['aux'=128,'occ'=4] {'occ'}, dimensions={0}, use_global_device_ids=true | all-gather | bytes 737280 | tf_op jit(solution)/shard_map/all_gather | solution.py:33
  69.0 0.1 broadcast_bitcast_fusion
  69.1 103.5 %all-to-all-done = bf16[128,18,384]{2,1,0:T(8,128)(2,1)} async-done(((bf16[128,18,384]{2,1,0:T(8,128)(2,1)}), bf16[128,18,384]{2,1,0:T(8,128)(2,1)}, u32[]{:S(2)}, u32[]{:S(2)}) %all-to-all-start) | async-done | bytes 1769504 | tf_op jit(solution)/shard_map/all_to_all | solution.py:28
  172.6 2.6 %reshape.21 = bf16[2304,384]{1,0:T(8,128)(2,1)S(1)} reshape(bf16[128,18,384]{2,1,0:T(8,128)(2,1)} %all-to-all-done) | data formatting | bytes 3538944 | tf_op jit(solution)/shard_map/reshape | solution.py:27
  175.3 0.0 copy-done
  175.3 0.3 fusion.3
  175.7 0.1 dot_general.13
  175.8 1.8 fusion
  (2 shorter events, 0.0 us)
Async XLA Ops:
  6.5 168.8 %copy-start = (bf16[18,2304]{1,0:T(8,128)(2,1)S(1)}, bf16[18,2304]{1,0:T(8,128)(2,1)}, u32[]{:S(2)}) copy-start(bf16[18,2304]{1,0:T(8,128)(2,1)} %param.7) | copy-start | bytes 248836
  6.5 32.8 %reduce-scatter.2.cloned.1.call-start = ((), (), s32[]{:S(2)}) async-start(), calls=%async_computation.2 | async-start | bytes 184320 | tf_op jit(solution)/shard_map/reduce_scatter | solution.py:24
  41.8 19.2 %copy-start.1 = (bf16[1536,48]{0,1:T(8,128)(2,1)S(1)}, bf16[1536,48]{0,1:T(8,128)(2,1)}, u32[]{:S(2)}) copy-start(bf16[1536,48]{0,1:T(8,128)(2,1)} %param.5) | copy-start | bytes 442372
  41.8 130.9 %all-to-all-start = ((bf16[128,18,384]{2,1,0:T(8,128)(2,1)}), bf16[128,18,384]{2,1,0:T(8,128)(2,1)}, u32[]{:S(2)}, u32[]{:S(2)}) async-start(bf16[128,18,384]{2,1,0:T(8,128)(2,1)} %stack.2), calls=%async_computation.1 | async-start | bytes 4718592 | tf_op jit(solution)/shard_map/all_to_all | solution.py:28
Sparse Core Ops, SparseCore 0:
  10.6 28.7 reduce-scatter.1
